TPU v7x, 256 devices: a whole 4x4x8 slice. The times are simulated.
256 devices in a mesh: gx: 8 (over z_hi, core), gy: 8 (over y, z_lo), gz: 4 (over x).
Axes of the slice: x: 4, y: 4, z: 8 (z_hi: 4, z_lo: 2; z = z_hi * 2 + z_lo), core: 2. Of those that a mesh axis runs over, the one named last changes fastest.
Arguments:
- pressure_prev: float32 [128, 192, 1024], P('gx', 'gy', 'gz'), may hold values from -6 to 6
- pressure_now: float32 [128, 192, 1024], P('gx', 'gy', 'gz'), may hold values from -6 to 6
- material: int32 [128, 192, 1024], P('gx', 'gy', 'gz'), may hold values from 0 to 7
- speed_table: float32 [8], replicated, may hold values from 0.05 to 0.32
- anchors: int32 [8, 8, 512], P('gx', 'gy', 'gz'), may hold values from 0 to 53496, as said below
- counts: int32 [8, 8, 4], P('gx', 'gy', 'gz'), may hold values from 64 to 128, as said below
- w_in: bfloat16 [512, 1024], replicated, may hold values from -0.25 to 0.25
- w_out: bfloat16 [1024, 512], replicated, may hold values from -0.1875 to 0.1875
Outputs:
- final_pressure: float32 [128, 192, 1024], P('gx', 'gy', 'gz')
- grad_in: float32 [512, 1024], P('gx')
- grad_out: float32 [1024, 512], P('gx')
Inputs may be any that keep to these rules, and one draw needn't show every extreme that they name: `anchors`: each entry is i * 24 * 256 + j * 256 + k with i <= 8, j <= 16, k <= 248, so every patch lies inside its brick; entries of a brick may repeat. The used slots of a brick are its first counts slots.
All inputs are finite; a program needn't handle non-finite values.
Results may differ from a plain program's by a relative error of at most 0.0017.
Values sent between devices are 32-bit elements; how exact they have to be, the bound alone decides.
A program may use at most 64 MiB of HBM per device.

v0:
```python
import jax
import jax.numpy as jnp
from jax import lax
from jax.sharding import PartitionSpec as P

STEPS = 8
PATCH = 8


def extended(x, sides, width):
    for axis, dim in sides:
        peers, length = (lax.axis_size(axis), x.shape[dim])
        up = [(i, (i + 1) % peers) for i in range(peers - 1)]
        down = [(j, i) for i, j in up]
        last = lax.slice_in_dim(x, length - width, length, axis=dim)
        first = lax.slice_in_dim(x, 0, width, axis=dim)
        before = lax.ppermute(last, axis, up)
        after = lax.ppermute(first, axis, down)
        x = jnp.concatenate([before, x, after], axis=dim)
    return x


def coefficient(material, speed_table):
    coef = jnp.zeros(material.shape, jnp.float32)
    for number in range(speed_table.shape[0]):
        coef = jnp.where(material == number, speed_table[number], coef)
    return coef


def update(prev, now, coef, padded):
    beside = padded[2:, 1:-1, 1:-1] + padded[:-2, 1:-1, 1:-1]
    beside = beside + padded[1:-1, 2:, 1:-1] + padded[1:-1, :-2, 1:-1]
    beside = beside + padded[1:-1, 1:-1, 2:] + padded[1:-1, 1:-1, :-2]
    return 2.0 * now - prev + coef * (beside - 6.0 * now)


def outer_sum(left, right):
    return lax.dot_general(
        left, right, (((0,), (0,)), ((), ())), preferred_element_type=jnp.float32
    )


def mlp_parts(inputs, targets, valid, total, w_in, w_out):
    scale = lax.rsqrt(jnp.mean(inputs * inputs, axis=-1, keepdims=True) + 1e-06)
    normed = (inputs * scale).astype(jnp.bfloat16)
    pre = jnp.dot(normed, w_in, preferred_element_type=jnp.float32)
    act = jax.nn.gelu(pre).astype(jnp.bfloat16)
    err = inputs + jnp.dot(act, w_out, preferred_element_type=jnp.float32) - targets
    dout = (2.0 * err * valid[:, None] / total).astype(jnp.bfloat16)
    dact = lax.dot_general(
        dout, w_out, (((1,), (1,)), ((), ())), preferred_element_type=jnp.float32
    )
    dpre = jax.vjp(jax.nn.gelu, pre)[1](dact)[0].astype(jnp.bfloat16)
    return (normed, act, dout, dpre)


def body(pressure_prev, pressure_now, material, speed_table, anchors, counts, w_in, w_out):
    coef = coefficient(material, speed_table)
    cells_x, cells_y, cells_z = pressure_now.shape
    prev, now = (pressure_prev, pressure_now)
    for step in range(STEPS):
        padded = extended(now, (("gx", 0), ("gy", 1), ("gz", 2)), 1)
        prev, now = (now, update(prev, now, coef, padded))
    local = anchors.reshape(-1)
    edge = jnp.arange(PATCH, dtype=jnp.int32)
    offsets = (
        edge[:, None, None] * (cells_y * cells_z)
        + edge[None, :, None] * cells_z
        + edge[None, None, :]
    ).reshape(-1)
    cell_index = local[:, None] + offsets[None, :]
    inputs = jnp.take(pressure_now.reshape(-1), cell_index, axis=0)
    targets = jnp.take(now.reshape(-1), cell_index, axis=0)
    slots = local.shape[0]
    used = counts.reshape(())
    total = lax.psum(used.astype(jnp.float32), ("gx", "gy", "gz"))
    valid = (jnp.arange(slots, dtype=jnp.int32) < used).astype(jnp.float32)
    normed, act, dout, dpre = mlp_parts(inputs, targets, valid, total, w_in, w_out)
    groups = lax.axis_size("gx")
    in_count = normed.shape[1] // groups
    out_count = act.shape[1] // groups
    full_in = outer_sum(normed, dpre)
    full_out = outer_sum(act, dout)
    summed_in, summed_out = lax.psum((full_in, full_out), ("gx", "gy", "gz"))
    position = lax.axis_index("gx")
    grad_in = lax.dynamic_slice_in_dim(summed_in, position * in_count, in_count, 0)
    grad_out = lax.dynamic_slice_in_dim(summed_out, position * out_count, out_count, 0)
    return (now, grad_in, grad_out)


def solution(mesh):
    return jax.shard_map(
        body,
        mesh=mesh,
        in_specs=(
            P("gx", "gy", "gz"),
            P("gx", "gy", "gz"),
            P("gx", "gy", "gz"),
            P(),
            P("gx", "gy", "gz"),
            P("gx", "gy", "gz"),
            P(),
            P(),
        ),
        out_specs=(P("gx", "gy", "gz"), P("gx", None), P("gx", None)),
        check_vma=False,
    )
```

profile of v0, /device:TPU:2, one launch (start us, length us, event | category | flops | bytes accessed | tf_op | source)
XLA Modules:
  0.0 1375.9 jit_solution(7897120378503387624)
XLA Ops:
  17.4 4.5 collective-permute-start.3
  36.6 5.7 fusion.70
  49.4 5.3 collective-permute-start.9
  58.4 3.9 collective-permute-start.11
  62.3 5.0 collective-permute-done.10
  69.2 5.7 fusion.62
  81.6 5.7 collective-permute-start.15
  91.0 4.0 collective-permute-start.17
  99.6 5.7 fusion.54
  106.6 6.7 collective-permute-start.19
  115.5 5.4 collective-permute-start.21
  124.5 3.9 collective-permute-start.23
  133.1 5.7 fusion.46
  140.1 7.6 collective-permute-start.25
  149.9 5.4 collective-permute-start.27
  158.9 3.9 collective-permute-start.29
  167.6 5.7 fusion.38
  174.5 7.6 collective-permute-start.31
  184.3 5.4 collective-permute-start.33
  194.0 3.9 collective-permute-start.35
  202.7 6.6 fusion.30
  210.6 7.3 collective-permute-start.37
  220.8 6.0 collective-permute-start.39
  227.1 362.7 %gather_fusion = f32[65536]{0:T(1024)S(1)} fusion(f32[98304]{0:T(1024)S(1)} %bitcast.25, s32[65536]{0:T(1024)S(1)} %broadcast_clamp_fusion), kind=kCustom, calls=%fused_computation.clone | custom fusion | bytes 786432 | tf_op jit(solution)/shard_map/jit(_take)/gather | solution.py:72
  601.6 6.5 fusion.22
  609.4 7.9 collective-permute-start.43
  619.4 4.9 collective-permute-start.45
  629.1 4.1 collective-permute-start.47
  633.2 86.1 %psum.21 = f32[]{:T(128)} all-reduce(f32[]{:T(128)S(6)} %convert_element_type.22), channel_id=1, replica_groups=mesh['gx'=8,'gy'=8,'gz'=4] {'gx','gy','gz'}, use_global_device_ids=true, to_apply=%region_1.3 | all-reduce | flops 1 | bytes 8 | tf_op jit(solution)/shard_map/psum | solution.py:76
  720.0 6.7 fusion.14
  727.0 362.7 %gather_fusion.1 = f32[65536]{0:T(1024)S(1)} fusion(f32[98304]{0:T(1024)S(1)} %bitcast.24, s32[65536]{0:T(1024)S(1)} %broadcast_clamp_fusion), kind=kCustom, calls=%fused_computation.1.clone | custom fusion | bytes 786432 | tf_op jit(solution)/shard_map/jit(_take)/gather | solution.py:73
  1095.1 270.6 %all-reduce.3.cloned.1.call-done = (f32[512,1024]{1,0:T(8,128)}, f32[1024,512]{1,0:T(8,128)}) async-done(((f32[512,1024]{1,0:T(8,128)}, f32[1024,512]{1,0:T(8,128)}), (f32[512,1024]{1,0:T(8,128)}, f32[1024,512]{1,0:T(8,128)})) %all-reduce.3.cloned.1.call-update) | async-done | bytes 4194320 | tf_op jit(solution)/shard_map/psum | solution.py:84
  (162 shorter events, 121.3 us)
Async XLA Ops:
  7.2 1358.4 %all-reduce.3.cloned.1.call-start = ((), (), s32[]{:S(2)}) async-start(), calls=%async_computation | async-start | bytes 8388608 | tf_op jit(solution)/shard_map/psum | solution.py:84
  23.6 10.2 collective-permute-start.4
  26.1 10.5 collective-permute-start.5
  56.4 10.9 collective-permute-start.10
  58.4 10.9 collective-permute-start.11
  80.3 7.0 collective-permute-start.14
  81.6 7.2 collective-permute-start.15
  89.1 8.7 collective-permute-start.16
  91.0 8.6 collective-permute-start.17
  105.3 8.0 collective-permute-start.18
  106.6 7.5 collective-permute-start.19
  122.6 8.6 collective-permute-start.22
  124.5 8.6 collective-permute-start.23
  138.8 8.9 collective-permute-start.24
  140.1 8.4 collective-permute-start.25
  157.0 8.6 collective-permute-start.28
  158.9 8.6 collective-permute-start.29
  173.2 8.9 collective-permute-start.30
  174.5 8.5 collective-permute-start.31
  192.1 8.8 collective-permute-start.34
  194.0 8.7 collective-permute-start.35
  209.3 8.8 collective-permute-start.36
  210.6 8.2 collective-permute-start.37
  219.5 370.4 %collective-permute-start.38 = (f32[18,1,256]{2,1,0:T(1,128)}, f32[18,1,256]{2,1,0:T(1,128)}, u32[]{:S(2)}, u32[]{:S(2)}) collective-permute-start(f32[18,1,256]{2,1,0:T(1,128)} %get-tuple-element.25), channel_id=1, source_target_pairs={{4,0},{8,4},{12,8},{16,12},{20,16},{24,20},{28,24},{5,1},{9,5},{13... | collective-permute-start | bytes 55304 | tf_op jit(solution)/shard_map/ppermute | solution.py:18
  220.8 369.1 %collective-permute-start.39 = (f32[18,1,256]{2,1,0:T(1,128)}, f32[18,1,256]{2,1,0:T(1,128)}, u32[]{:S(2)}, u32[]{:S(2)}) collective-permute-start(f32[18,1,256]{2,1,0:T(1,128)} %get-tuple-element.24), channel_id=1, source_target_pairs={{0,4},{4,8},{8,12},{12,16},{16,20},{20,24},{24,28},{1,5},{5,9},{9,... | collective-permute-start | bytes 55304 | tf_op jit(solution)/shard_map/ppermute | solution.py:17
  590.9 8.7 collective-permute-start.40
  593.0 8.6 collective-permute-start.41
  608.1 9.2 collective-permute-start.42
  609.4 8.8 collective-permute-start.43
  618.1 8.0 collective-permute-start.44
  627.2 92.1 %collective-permute-start.46 = (f32[18,26,1]{2,1,0:T(8,128)}, f32[18,26,1]{2,1,0:T(8,128)S(1)}, u32[]{:S(2)}, u32[]{:S(2)}) collective-permute-start(f32[18,26,1]{2,1,0:T(8,128)} %get-tuple-element.6), channel_id=1, source_target_pairs={{1,0},{2,1},{3,2},{5,4},{6,5},{7,6},{9,8},{10,9},{11,10},{13,12},{... | collective-permute-start | bytes 5624 | tf_op jit(solution)/shard_map/ppermute | solution.py:18
  629.1 90.9 %collective-permute-start.47 = (f32[18,26,1]{2,1,0:T(8,128)}, f32[18,26,1]{2,1,0:T(8,128)}, u32[]{:S(2)}, u32[]{:S(2)}) collective-permute-start(f32[18,26,1]{2,1,0:T(8,128)} %get-tuple-element.7), channel_id=1, source_target_pairs={{0,1},{1,2},{2,3},{4,5},{5,6},{6,7},{8,9},{9,10},{10,11},{12,13},{... | collective-permute-start | bytes 5624 | tf_op jit(solution)/shard_map/ppermute | solution.py:17
  (31 other events, 2823.8 us)
Sparse Core Ops, SparseCore 0:
  1095.2 270.4 all-reduce.2
where the time goes:
time: 1380 us
  local copies, waits for them, and re-layouts  735 us (53%)
  waiting for transfers between devices  325 us (24%)
  starting transfers between devices  156 us (11%)
  blocking collectives  86.1 us (6%)
  other arithmetic  50.9 us (4%)
  between operations  15.7 us (1%)
    gather x2, local copies, waits for them, and re-layouts, body(): targets = jnp.take(now.reshape(-1), cell_index, axis=0)  363 us
    gather x2, local copies, waits for them, and re-layouts, body(): inputs = jnp.take(pressure_now.reshape(-1), cell_index, axis=0)  363 us
    psum x1, waiting for transfers between devices, body(): summed_in, summed_out = lax.psum((full_in, full_out), ('gx', 'gy', 'gz'))  271 us
    ppermute x24, starting transfers between devices, extended(): before = lax.ppermute(last, axis, up)  120 us
    psum x1, blocking collectives, body(): total = lax.psum(used.astype(jnp.float32), ('gx', 'gy', 'gz'))  86.1 us
    add x8, other arithmetic, update(): return 2.0 * now - prev + coef * (beside - 6.0 * now)  48.1 us
    ppermute x24, starting transfers between devices, extended(): after = lax.ppermute(first, axis, down)  36.7 us
    ppermute x24, waiting for transfers between devices, extended(): before = lax.ppermute(last, axis, up)  28.2 us
  transfers between devices with their start and end apart: 49, of which 29 were waited for; matrix products, arithmetic and copies ran while one was open for 27% of the time, Pallas kernels for 0%

commit v1 on v0

--- a/solution.py
+++ b/solution.py
@@ -1,3 +1,4 @@
+import functools
 import jax
 import jax.numpy as jnp
 from jax import lax
@@ -5,6 +6,14 @@
 
 STEPS = 8
 PATCH = 8
+
+
+def close_state_on(content, mesh_name, group_axis):
+    big = lax.psum(content, mesh_name)
+    return lax.psum(big, group_axis)
+
+
+supply_all_steps_all = functools.partial(close_state_on, mesh_name="gx", group_axis=("gy", "gz"))
 
 
 def extended(x, sides, width):
@@ -81,7 +90,7 @@
     out_count = act.shape[1] // groups
     full_in = outer_sum(normed, dpre)
     full_out = outer_sum(act, dout)
-    summed_in, summed_out = lax.psum((full_in, full_out), ("gx", "gy", "gz"))
+    summed_in, summed_out = supply_all_steps_all((full_in, full_out))
     position = lax.axis_index("gx")
     grad_in = lax.dynamic_slice_in_dim(summed_in, position * in_count, in_count, 0)
     grad_out = lax.dynamic_slice_in_dim(summed_out, position * out_count, out_count, 0)

time: 1380 us -> 1550 us (1.12)
  waiting for transfers between devices: 325 us -> 500 us
    psum x1 -> x2, waiting for transfers between devices: 271 us -> 445 us  [the longest x1 329 us: close_state_on(): return lax.psum(big, group_axis)]
  transfers between devices with their start and end apart: 49 -> 50, of which waited for: 29 -> 30; matrix products, arithmetic and copies ran while one was open for 27% -> 24% of each run, Pallas kernels for 0% -> 0%
where the time goes in v1:
time: 1550 us
  local copies, waits for them, and re-layouts  735 us (47%)
  waiting for transfers between devices  500 us (32%)
  starting transfers between devices  156 us (10%)
  blocking collectives  86.1 us (6%)
  other arithmetic  49.8 us (3%)
  between operations  15.7 us (1%)
    gather x2, local copies, waits for them, and re-layouts, body(): inputs = jnp.take(pressure_now.reshape(-1), cell_index, axis=0)  363 us
    gather x2, local copies, waits for them, and re-layouts, body(): targets = jnp.take(now.reshape(-1), cell_index, axis=0)  363 us
    psum x1, waiting for transfers between devices, close_state_on(): return lax.psum(big, group_axis)  329 us
    ppermute x24, starting transfers between devices, extended(): before = lax.ppermute(last, axis, up)  120 us
    psum x1, waiting for transfers between devices, close_state_on(): big = lax.psum(content, mesh_name)  116 us
    psum x1, blocking collectives, body(): total = lax.psum(used.astype(jnp.float32), ('gx', 'gy', 'gz'))  86.1 us
    add x8, other arithmetic, update(): return 2.0 * now - prev + coef * (beside - 6.0 * now)  47 us
    ppermute x24, starting transfers between devices, extended(): after = lax.ppermute(first, axis, down)  36.7 us
  transfers between devices with their start and end apart: 50, of which 30 were waited for; matrix products, arithmetic and copies ran while one was open for 24% of the time, Pallas kernels for 0%

profile of v1, /device:TPU:2, one launch (start us, length us, event | category | flops | bytes accessed | tf_op | source)
XLA Modules:
  0.0 1549.6 jit_solution(10346805802894425387)
XLA Ops:
  17.4 4.5 collective-permute-start.3
  36.6 5.5 fusion.70
  49.2 5.3 collective-permute-start.9
  58.2 3.9 collective-permute-start.11
  62.2 5.0 collective-permute-done.10
  69.1 5.5 fusion.62
  81.4 5.7 collective-permute-start.15
  90.7 4.0 collective-permute-start.17
  99.4 5.5 fusion.54
  106.2 6.7 collective-permute-start.19
  115.1 5.4 collective-permute-start.21
  132.7 5.5 fusion.46
  139.6 7.6 collective-permute-start.25
  149.4 5.4 collective-permute-start.27
  167.0 5.5 fusion.38
  173.9 7.6 collective-permute-start.31
  183.7 5.4 collective-permute-start.33
  193.4 3.9 collective-permute-start.35
  202.1 6.5 fusion.30
  209.9 7.3 collective-permute-start.37
  220.0 6.0 collective-permute-start.39
  226.3 362.7 %gather_fusion = f32[65536]{0:T(1024)S(1)} fusion(f32[98304]{0:T(1024)S(1)} %bitcast.25, s32[65536]{0:T(1024)S(1)} %broadcast_clamp_fusion), kind=kCustom, calls=%fused_computation.clone | custom fusion | bytes 786432 | tf_op jit(solution)/shard_map/jit(_take)/gather | solution.py:81
  592.2 3.9 collective-permute-start.41
  600.8 6.3 fusion.22
  608.5 7.9 collective-permute-start.43
  618.5 4.8 collective-permute-start.45
  628.2 4.1 collective-permute-start.47
  632.3 86.1 %psum.35 = f32[]{:T(128)} all-reduce(f32[]{:T(128)S(6)} %convert_element_type.22), channel_id=1, replica_groups=mesh['gx'=8,'gy'=8,'gz'=4] {'gx','gy','gz'}, use_global_device_ids=true, to_apply=%region_1.3 | all-reduce | flops 1 | bytes 8 | tf_op jit(solution)/shard_map/psum | solution.py:85
  719.1 6.5 fusion.14
  725.9 362.7 %gather_fusion.1 = f32[65536]{0:T(1024)S(1)} fusion(f32[98304]{0:T(1024)S(1)} %bitcast.24, s32[65536]{0:T(1024)S(1)} %broadcast_clamp_fusion), kind=kCustom, calls=%fused_computation.1.clone | custom fusion | bytes 786432 | tf_op jit(solution)/shard_map/jit(_take)/gather | solution.py:82
  1094.1 116.4 %all-reduce.7.cloned.1.call-done = (f32[512,1024]{1,0:T(8,128)}, f32[1024,512]{1,0:T(8,128)}) async-done(((f32[512,1024]{1,0:T(8,128)}, f32[1024,512]{1,0:T(8,128)}), (f32[512,1024]{1,0:T(8,128)}, f32[1024,512]{1,0:T(8,128)})) %all-reduce.7.cloned.1.call-update) | async-done | bytes 4194320 | tf_op jit(solution)/shard_map/psum | solution.py:12
  1210.5 328.9 %all-reduce.5.cloned.1.call-done = (f32[512,1024]{1,0:T(8,128)}, f32[1024,512]{1,0:T(8,128)}) async-done(((f32[512,1024]{1,0:T(8,128)}, f32[1024,512]{1,0:T(8,128)}), (f32[512,1024]{1,0:T(8,128)}, f32[1024,512]{1,0:T(8,128)})) %all-reduce.5.cloned.1.call-update) | async-done | bytes 4194320 | tf_op jit(solution)/shard_map/psum | solution.py:13
  (165 shorter events, 125.2 us)
Async XLA Ops:
  7.2 1203.3 %all-reduce.7.cloned.1.call-start = ((), (), s32[]{:S(2)}) async-start(), calls=%async_computation.1 | async-start | bytes 8388608 | tf_op jit(solution)/shard_map/psum | solution.py:12
  23.6 10.2 collective-permute-start.4
  26.1 10.5 collective-permute-start.5
  56.3 10.9 collective-permute-start.10
  58.2 10.9 collective-permute-start.11
  81.4 7.2 collective-permute-start.15
  88.8 8.7 collective-permute-start.16
  90.7 8.6 collective-permute-start.17
  104.9 8.0 collective-permute-start.18
  106.2 7.5 collective-permute-start.19
  122.2 8.6 collective-permute-start.22
  124.1 8.6 collective-permute-start.23
  138.3 8.9 collective-permute-start.24
  139.6 8.4 collective-permute-start.25
  156.5 8.6 collective-permute-start.28
  158.4 8.6 collective-permute-start.29
  172.6 8.9 collective-permute-start.30
  173.9 8.5 collective-permute-start.31
  191.4 8.8 collective-permute-start.34
  193.4 8.7 collective-permute-start.35
  208.6 8.8 collective-permute-start.36
  209.9 8.2 collective-permute-start.37
  218.7 370.4 %collective-permute-start.38 = (f32[18,1,256]{2,1,0:T(1,128)}, f32[18,1,256]{2,1,0:T(1,128)}, u32[]{:S(2)}, u32[]{:S(2)}) collective-permute-start(f32[18,1,256]{2,1,0:T(1,128)} %get-tuple-element.27), channel_id=1, source_target_pairs={{4,0},{8,4},{12,8},{16,12},{20,16},{24,20},{28,24},{5,1},{9,5},{13... | collective-permute-start | bytes 55304 | tf_op jit(solution)/shard_map/ppermute | solution.py:27
  220.0 369.1 %collective-permute-start.39 = (f32[18,1,256]{2,1,0:T(1,128)}, f32[18,1,256]{2,1,0:T(1,128)}, u32[]{:S(2)}, u32[]{:S(2)}) collective-permute-start(f32[18,1,256]{2,1,0:T(1,128)} %get-tuple-element.26), channel_id=1, source_target_pairs={{0,4},{4,8},{8,12},{12,16},{16,20},{20,24},{24,28},{1,5},{5,9},{9,... | collective-permute-start | bytes 55304 | tf_op jit(solution)/shard_map/ppermute | solution.py:26
  590.1 8.7 collective-permute-start.40
  592.2 8.6 collective-permute-start.41
  607.2 9.2 collective-permute-start.42
  608.5 8.8 collective-permute-start.43
  617.2 8.0 collective-permute-start.44
  626.3 92.1 %collective-permute-start.46 = (f32[18,26,1]{2,1,0:T(8,128)}, f32[18,26,1]{2,1,0:T(8,128)S(1)}, u32[]{:S(2)}, u32[]{:S(2)}) collective-permute-start(f32[18,26,1]{2,1,0:T(8,128)} %get-tuple-element.8), channel_id=1, source_target_pairs={{1,0},{2,1},{3,2},{5,4},{6,5},{7,6},{9,8},{10,9},{11,10},{13,12},{... | collective-permute-start | bytes 5624 | tf_op jit(solution)/shard_map/ppermute | solution.py:27
  628.2 91.0 %collective-permute-start.47 = (f32[18,26,1]{2,1,0:T(8,128)}, f32[18,26,1]{2,1,0:T(8,128)}, u32[]{:S(2)}, u32[]{:S(2)}) collective-permute-start(f32[18,26,1]{2,1,0:T(8,128)} %get-tuple-element.9), channel_id=1, source_target_pairs={{0,1},{1,2},{2,3},{4,5},{5,6},{6,7},{8,9},{9,10},{10,11},{12,13},{... | collective-permute-start | bytes 5624 | tf_op jit(solution)/shard_map/ppermute | solution.py:26
  1094.0 445.4 %all-reduce.5.cloned.1.call-start = ((), (), s32[]{:S(2)}) async-start(), calls=%async_computation | async-start | bytes 8388608 | tf_op jit(solution)/shard_map/psum | solution.py:13
  (32 other events, 2829.5 us)
Sparse Core Ops, SparseCore 0:
  1094.1 116.2 all-reduce.6
  1213.2 326.1 all-reduce.4
